TPU v7x, 256 devices: a whole 4x4x8 slice. The times are simulated.
256 devices in a mesh: ctx: 64 (over x, z, core), head: 4 (over y).
Axes of the slice: x: 4, y: 4, z: 8, core: 2. Of those that a mesh axis runs over, the one named last changes fastest.
Arguments:
- mixer_input: bfloat16 [32768, 4096], P('ctx', 'head'), may hold values from -61 to 61
- gate_input: bfloat16 [32768, 4096], P('ctx', 'head'), may hold values from -7.5 to 7.5
- write_vecs: bfloat16 [32768, 128], P('ctx'), may hold values from -0.8984375 to 0.8984375
- read_vecs: bfloat16 [32768, 128], P('ctx'), may hold values from -0.8984375 to 0.8984375
- log_decay: float32 [64, 32768], P('head', 'ctx'), may hold values from -0.76 to 0
- doc_start: int32 [32768], P('ctx'), may hold values from 0 to 1, as said below
- live_mask: int32 [32768], P('ctx'), may hold values from 0 to 1, as said below
- skip_gain: float32 [64], P('head'), may hold values from 0.5 to 2
- norm_gain: float32 [4096], P('head'), may hold values from 0.25 to 1.75
- residual: bfloat16 [32768, 2048], P('ctx', 'head'), may hold values from -61 to 61
- out_weight: bfloat16 [4096, 2048], P(('head', 'ctx')), may hold values from -0.09375 to 0.09375
- mlp_gain: float32 [2048], replicated, may hold values from 0.25 to 1.75
- gate_weight: bfloat16 [2048, 4096], P('ctx', 'head'), may hold values from -0.125 to 0.125
- up_weight: bfloat16 [2048, 4096], P('ctx', 'head'), may hold values from -0.125 to 0.125
- down_weight: bfloat16 [4096, 2048], P(('head', 'ctx')), may hold values from -0.09375 to 0.09375
Outputs:
- mixed: bfloat16 [32768, 2048], P('ctx', 'head')
Inputs may be any that keep to these rules, and one draw needn't show every extreme that they name: `doc_start`: documents begin only at the first token of a group of 256; the window's first token begins one; a document spans at most 16 groups, and some document spans exactly that many. `live_mask`: the 0 entries are the tokens after a document's last real token, all within its last group; every document has a real token.
All inputs are finite; a program needn't handle non-finite values.
Results may differ from a plain program's by a relative error of at most 0.007.
Values may be sent and summed in bfloat16 or wider, within the bound.
No kernel may reach another device: no remote copies, remote signals or barrier semaphores. Data moves between devices by JAX's collectives and lax.ppermute only.
A program may use at most 128 MiB of HBM per device.

v0:
```python
import jax
import jax.numpy as jnp
from jax import lax
from jax.sharding import PartitionSpec as P

HDIM = 64
STATE = 128
GROUP = 256
DOC_GROUPS = 16
INNER = 4096
EPS = 1e-05


def passed_along(array, axis, by):
    peers = lax.axis_size(axis)
    pairs = [(i, i + by) for i in range(peers) if 0 <= i + by < peers]
    return lax.ppermute(array, axis, pairs)


def sent_together(arrays, axis, dim, along):
    widths = [a.shape[along] for a in arrays]
    both = jnp.concatenate(arrays, axis=along)
    filled = lax.all_gather(both, axis, axis=dim, tiled=True)
    return tuple(jnp.split(filled, [sum(widths[:k]) for k in range(1, len(widths))], axis=along))


def group_core(masked, write_group, read_group, log_group, start_group, skip_gain):
    positions = jnp.arange(GROUP)
    log_sums = jnp.cumsum(log_group, axis=1)
    doc_index = jnp.cumsum(start_group)
    same_doc = (doc_index[:, None] == doc_index[None, :]) & (
        positions[:, None] >= positions[None, :]
    )
    scores = jnp.dot(read_group, write_group.T, preferred_element_type=jnp.float32)
    log_gaps = jnp.where(same_doc[None], log_sums[:, :, None] - log_sums[:, None, :], 0.0)
    weights = jnp.where(same_doc[None], scores[None] * jnp.exp(log_gaps), 0.0).astype(jnp.bfloat16)
    per_head = masked.reshape(GROUP, -1, HDIM)
    intra_out = jnp.einsum("hij,jhp->ihp", weights, per_head, preferred_element_type=jnp.float32)
    tail_wts = (
        jnp.exp(log_sums[:, -1:] - log_sums)
        * (doc_index == doc_index[-1]).astype(jnp.float32)[None]
    )
    weighted = (write_group.astype(jnp.float32)[None] * tail_wts[:, :, None]).astype(jnp.bfloat16)
    local_state = jnp.einsum("hjn,jhp->hnp", weighted, per_head, preferred_element_type=jnp.float32)
    reach_wts = jnp.exp(log_sums) * (doc_index == 0).astype(jnp.float32)[None]
    decay_all = jnp.exp(log_sums[:, -1]) * (doc_index[-1] == 0).astype(jnp.float32)
    direct = intra_out + skip_gain[None, :, None] * per_head.astype(jnp.float32)
    return (direct, local_state, reach_wts, decay_all)


def shards(
    mixer_input,
    gate_input,
    write_vecs,
    read_vecs,
    log_decay,
    doc_start,
    live_mask,
    skip_gain,
    norm_gain,
    residual,
    out_weight,
    mlp_gain,
    gate_weight,
    up_weight,
    down_weight,
):
    tok_rows = mixer_input.shape[0]
    group_total = tok_rows // GROUP
    head_count = log_decay.shape[0]
    masked = mixer_input * live_mask.astype(jnp.bfloat16)[:, None]
    read_groups = read_vecs.reshape(group_total, GROUP, -1)
    group_data = (
        masked.reshape(group_total, GROUP, -1),
        write_vecs.reshape(group_total, GROUP, -1),
        read_groups,
        log_decay.reshape(head_count, group_total, GROUP).transpose(1, 0, 2),
        doc_start.reshape(group_total, GROUP),
    )

    def group_step(pieces):
        return group_core(pieces[0], pieces[1], pieces[2], pieces[3], pieces[4], skip_gain)

    directs, local_parts, reaches, decays = lax.map(group_step, group_data)
    run_state = jnp.zeros((head_count, STATE, HDIM), jnp.float32)
    run_factor = jnp.ones((head_count,), jnp.float32)
    before = []
    factors = []
    for group_id in range(group_total):
        before.append(run_state)
        factors.append(run_factor)
        run_state = decays[group_id][:, None, None] * run_state + local_parts[group_id]
        run_factor = run_factor * decays[group_id]
    hop_count = min(DOC_GROUPS // group_total + 1, lax.axis_size("ctx") - 1)

    def hop(hop_id, arriving):
        return passed_along(run_factor[:, None, None] * arriving + run_state, "ctx", 1)

    incoming = lax.fori_loop(0, hop_count, hop, jnp.zeros((head_count, STATE, HDIM), jnp.float32))
    outputs = []
    for group_id in range(group_total):
        inner_state = (factors[group_id][:, None, None] * incoming + before[group_id]).astype(
            jnp.bfloat16
        )
        crossed = jnp.einsum(
            "in,hnp->ihp", read_groups[group_id], inner_state, preferred_element_type=jnp.float32
        )
        outputs.append(directs[group_id] + crossed * reaches[group_id].T[:, :, None])
    output = jnp.concatenate(outputs, axis=0).reshape(tok_rows, -1)
    gated = output * jax.nn.silu(gate_input.astype(jnp.float32))
    squares = lax.psum(jnp.sum(gated * gated, axis=1), "head")
    normed = (gated * lax.rsqrt(squares / INNER + EPS)[:, None] * norm_gain).astype(jnp.bfloat16)
    width = out_weight.shape[1]
    columns = normed
    projected = jnp.dot(
        columns,
        lax.all_gather(out_weight, "ctx", axis=0, tiled=True),
        preferred_element_type=jnp.float32,
    )
    slice_width = residual.shape[1]
    offset = lax.axis_index("head") * slice_width
    placed = lax.dynamic_update_slice_in_dim(
        jnp.zeros((tok_rows, width), jnp.float32), residual.astype(jnp.float32), offset, 1
    )
    hidden_full = lax.psum(projected + placed, "head").astype(jnp.bfloat16)
    hidden_wide = hidden_full.astype(jnp.float32)
    row_scale = lax.rsqrt(jnp.mean(hidden_wide * hidden_wide, axis=1) + EPS)
    scaled = (hidden_wide * row_scale[:, None] * mlp_gain).astype(jnp.bfloat16)
    hidden = lax.dynamic_slice_in_dim(hidden_full, offset, slice_width, 1)
    pieces = sent_together((gate_weight, up_weight), "ctx", 0, 1)
    columns = scaled
    gate_out = jnp.dot(columns, pieces[0], preferred_element_type=jnp.float32)
    up_out = jnp.dot(columns, pieces[1], preferred_element_type=jnp.float32)
    act = (jax.nn.silu(gate_out) * up_out).astype(jnp.bfloat16)
    columns = act
    down_out = jnp.dot(
        columns,
        lax.all_gather(down_weight, "ctx", axis=0, tiled=True),
        preferred_element_type=jnp.float32,
    )
    mlp_part = lax.psum_scatter(
        down_out.astype(jnp.bfloat16), "head", scatter_dimension=1, tiled=True
    ).astype(jnp.float32)
    return (
        live_mask.astype(jnp.float32)[:, None] * (hidden.astype(jnp.float32) + mlp_part)
    ).astype(jnp.bfloat16)


def solution(mesh):
    return jax.shard_map(
        shards,
        mesh=mesh,
        in_specs=(
            P("ctx", "head"),
            P("ctx", "head"),
            P("ctx", None),
            P("ctx", None),
            P("head", "ctx"),
            P("ctx"),
            P("ctx"),
            P("head"),
            P("head"),
            P("ctx", "head"),
            P(("head", "ctx"), None),
            P(),
            P("ctx", "head"),
            P("ctx", "head"),
            P(("head", "ctx"), None),
        ),
        out_specs=P("ctx", "head"),
        check_vma=False,
    )
```

profile of v0, /device:TPU:1, one launch (start us, length us, event | category | flops | bytes accessed | tf_op | source)
XLA Modules:
  0.0 326.1 jit_solution(116184803706498684)
XLA Ops:
  15.1 27.7 %while.26 = (s32[]{:T(128)}, f32[2,256,16,64]{1,3,2,0:T(8,128)}, f32[2,16,128,64]{2,3,1,0:T(8,128)S(1)}, f32[2,16,256]{2,1,0:T(8,128)}, f32[2,16]{1,0:T(2,128)},...) while((s32[]{:T(128)}, f32[2,256,16,64]{1,3,2,0:T(8,128)}, ...), condition=%wide.region_5.6_spmd, body=%wide.region_0.5_spmd.sunk | while | flops 225981504 | bytes 7140167 | solution.py:84
  21.9 3.2 fusion.76
  35.7 3.2 fusion.76
  45.2 110.8 %while.27 = (s32[]{:T(128)}, f32[16,128,64]{1,2,0:T(8,128)S(1)}, f32[16]{0:T(128)S(1)}, f32[16,128,64]{1,2,0:T(8,128)S(1)}, s32[]{:T(128)}) while((s32[]{:T(128)}, f32[16,128,64]{1,2,0:T(8,128)S(1)}, f32[16]{0:T(128)S(1)}, f32[16,128,64]{1,2,0:T(8,128)S(1)}, s32[]{:T(128)}) %tuple.50), condition=%wide.region_7.8_spmd, body=%wide.region_6.7_spmd.sunk | while | flops 262146 | bytes 3670181 | solution.py:99
  45.4 4.9 %collective-permute-start = (f32[16,128,64]{1,2,0:T(8,128)S(1)}, f32[16,128,64]{1,2,0:T(8,128)S(1)}, u32[]{:S(2)}, u32[]{:S(2)}) collective-permute-start(f32[16,128,64]{1,2,0:T(8,128)S(1)} %multiply_add_fusion.2), channel_id=1, source_target_pairs={{0,4},{4,8},{8,12},{12,16},{16,20},{20,24},{24,28},{28,32},{32,36}... | collective-permute-start | bytes 1572872 | tf_op jit(solution)/shard_map/while/body/eval_jaxpr/ppermute | solution.py:17
  50.3 6.2 %collective-permute-done = f32[16,128,64]{1,2,0:T(8,128)S(1)} collective-permute-done((f32[16,128,64]{1,2,0:T(8,128)S(1)}, f32[16,128,64]{1,2,0:T(8,128)S(1)}, u32[]{:S(2)}, u32[]{:S(2)}) %collective-permute-start) | collective-permute-done | bytes 524320 | tf_op jit(solution)/shard_map/while/body/eval_jaxpr/ppermute | solution.py:17
  56.7 4.4 %collective-permute-start = (f32[16,128,64]{1,2,0:T(8,128)S(1)}, f32[16,128,64]{1,2,0:T(8,128)S(1)}, u32[]{:S(2)}, u32[]{:S(2)}) collective-permute-start(f32[16,128,64]{1,2,0:T(8,128)S(1)} %multiply_add_fusion.2), channel_id=1, source_target_pairs={{0,4},{4,8},{8,12},{12,16},{16,20},{20,24},{24,28},{28,32},{32,36}... | collective-permute-start | bytes 1572872 | tf_op jit(solution)/shard_map/while/body/eval_jaxpr/ppermute | solution.py:17
  61.1 8.1 %collective-permute-done = f32[16,128,64]{1,2,0:T(8,128)S(1)} collective-permute-done((f32[16,128,64]{1,2,0:T(8,128)S(1)}, f32[16,128,64]{1,2,0:T(8,128)S(1)}, u32[]{:S(2)}, u32[]{:S(2)}) %collective-permute-start) | collective-permute-done | bytes 524320 | tf_op jit(solution)/shard_map/while/body/eval_jaxpr/ppermute | solution.py:17
  69.3 4.5 %collective-permute-start = (f32[16,128,64]{1,2,0:T(8,128)S(1)}, f32[16,128,64]{1,2,0:T(8,128)S(1)}, u32[]{:S(2)}, u32[]{:S(2)}) collective-permute-start(f32[16,128,64]{1,2,0:T(8,128)S(1)} %multiply_add_fusion.2), channel_id=1, source_target_pairs={{0,4},{4,8},{8,12},{12,16},{16,20},{20,24},{24,28},{28,32},{32,36}... | collective-permute-start | bytes 1572872 | tf_op jit(solution)/shard_map/while/body/eval_jaxpr/ppermute | solution.py:17
  73.8 10.7 %collective-permute-done = f32[16,128,64]{1,2,0:T(8,128)S(1)} collective-permute-done((f32[16,128,64]{1,2,0:T(8,128)S(1)}, f32[16,128,64]{1,2,0:T(8,128)S(1)}, u32[]{:S(2)}, u32[]{:S(2)}) %collective-permute-start) | collective-permute-done | bytes 524320 | tf_op jit(solution)/shard_map/while/body/eval_jaxpr/ppermute | solution.py:17
  84.6 4.4 %collective-permute-start = (f32[16,128,64]{1,2,0:T(8,128)S(1)}, f32[16,128,64]{1,2,0:T(8,128)S(1)}, u32[]{:S(2)}, u32[]{:S(2)}) collective-permute-start(f32[16,128,64]{1,2,0:T(8,128)S(1)} %multiply_add_fusion.2), channel_id=1, source_target_pairs={{0,4},{4,8},{8,12},{12,16},{16,20},{20,24},{24,28},{28,32},{32,36}... | collective-permute-start | bytes 1572872 | tf_op jit(solution)/shard_map/while/body/eval_jaxpr/ppermute | solution.py:17
  89.0 6.4 %collective-permute-done = f32[16,128,64]{1,2,0:T(8,128)S(1)} collective-permute-done((f32[16,128,64]{1,2,0:T(8,128)S(1)}, f32[16,128,64]{1,2,0:T(8,128)S(1)}, u32[]{:S(2)}, u32[]{:S(2)}) %collective-permute-start) | collective-permute-done | bytes 524320 | tf_op jit(solution)/shard_map/while/body/eval_jaxpr/ppermute | solution.py:17
  95.4 4.4 %collective-permute-start = (f32[16,128,64]{1,2,0:T(8,128)S(1)}, f32[16,128,64]{1,2,0:T(8,128)S(1)}, u32[]{:S(2)}, u32[]{:S(2)}) collective-permute-start(f32[16,128,64]{1,2,0:T(8,128)S(1)} %multiply_add_fusion.2), channel_id=1, source_target_pairs={{0,4},{4,8},{8,12},{12,16},{16,20},{20,24},{24,28},{28,32},{32,36}... | collective-permute-start | bytes 1572872 | tf_op jit(solution)/shard_map/while/body/eval_jaxpr/ppermute | solution.py:17
  99.8 6.1 %collective-permute-done = f32[16,128,64]{1,2,0:T(8,128)S(1)} collective-permute-done((f32[16,128,64]{1,2,0:T(8,128)S(1)}, f32[16,128,64]{1,2,0:T(8,128)S(1)}, u32[]{:S(2)}, u32[]{:S(2)}) %collective-permute-start) | collective-permute-done | bytes 524320 | tf_op jit(solution)/shard_map/while/body/eval_jaxpr/ppermute | solution.py:17
  106.1 4.4 %collective-permute-start = (f32[16,128,64]{1,2,0:T(8,128)S(1)}, f32[16,128,64]{1,2,0:T(8,128)S(1)}, u32[]{:S(2)}, u32[]{:S(2)}) collective-permute-start(f32[16,128,64]{1,2,0:T(8,128)S(1)} %multiply_add_fusion.2), channel_id=1, source_target_pairs={{0,4},{4,8},{8,12},{12,16},{16,20},{20,24},{24,28},{28,32},{32,36}... | collective-permute-start | bytes 1572872 | tf_op jit(solution)/shard_map/while/body/eval_jaxpr/ppermute | solution.py:17
  110.5 7.8 %collective-permute-done = f32[16,128,64]{1,2,0:T(8,128)S(1)} collective-permute-done((f32[16,128,64]{1,2,0:T(8,128)S(1)}, f32[16,128,64]{1,2,0:T(8,128)S(1)}, u32[]{:S(2)}, u32[]{:S(2)}) %collective-permute-start) | collective-permute-done | bytes 524320 | tf_op jit(solution)/shard_map/while/body/eval_jaxpr/ppermute | solution.py:17
  118.3 4.4 %collective-permute-start = (f32[16,128,64]{1,2,0:T(8,128)S(1)}, f32[16,128,64]{1,2,0:T(8,128)S(1)}, u32[]{:S(2)}, u32[]{:S(2)}) collective-permute-start(f32[16,128,64]{1,2,0:T(8,128)S(1)} %multiply_add_fusion.2), channel_id=1, source_target_pairs={{0,4},{4,8},{8,12},{12,16},{16,20},{20,24},{24,28},{28,32},{32,36}... | collective-permute-start | bytes 1572872 | tf_op jit(solution)/shard_map/while/body/eval_jaxpr/ppermute | solution.py:17
  122.7 7.6 %collective-permute-done = f32[16,128,64]{1,2,0:T(8,128)S(1)} collective-permute-done((f32[16,128,64]{1,2,0:T(8,128)S(1)}, f32[16,128,64]{1,2,0:T(8,128)S(1)}, u32[]{:S(2)}, u32[]{:S(2)}) %collective-permute-start) | collective-permute-done | bytes 524320 | tf_op jit(solution)/shard_map/while/body/eval_jaxpr/ppermute | solution.py:17
  130.4 4.4 %collective-permute-start = (f32[16,128,64]{1,2,0:T(8,128)S(1)}, f32[16,128,64]{1,2,0:T(8,128)S(1)}, u32[]{:S(2)}, u32[]{:S(2)}) collective-permute-start(f32[16,128,64]{1,2,0:T(8,128)S(1)} %multiply_add_fusion.2), channel_id=1, source_target_pairs={{0,4},{4,8},{8,12},{12,16},{16,20},{20,24},{24,28},{28,32},{32,36}... | collective-permute-start | bytes 1572872 | tf_op jit(solution)/shard_map/while/body/eval_jaxpr/ppermute | solution.py:17
  134.8 6.1 %collective-permute-done = f32[16,128,64]{1,2,0:T(8,128)S(1)} collective-permute-done((f32[16,128,64]{1,2,0:T(8,128)S(1)}, f32[16,128,64]{1,2,0:T(8,128)S(1)}, u32[]{:S(2)}, u32[]{:S(2)}) %collective-permute-start) | collective-permute-done | bytes 524320 | tf_op jit(solution)/shard_map/while/body/eval_jaxpr/ppermute | solution.py:17
  141.1 4.4 %collective-permute-start = (f32[16,128,64]{1,2,0:T(8,128)S(1)}, f32[16,128,64]{1,2,0:T(8,128)S(1)}, u32[]{:S(2)}, u32[]{:S(2)}) collective-permute-start(f32[16,128,64]{1,2,0:T(8,128)S(1)} %multiply_add_fusion.2), channel_id=1, source_target_pairs={{0,4},{4,8},{8,12},{12,16},{16,20},{20,24},{24,28},{28,32},{32,36}... | collective-permute-start | bytes 1572872 | tf_op jit(solution)/shard_map/while/body/eval_jaxpr/ppermute | solution.py:17
  145.5 10.6 %collective-permute-done = f32[16,128,64]{1,2,0:T(8,128)S(1)} collective-permute-done((f32[16,128,64]{1,2,0:T(8,128)S(1)}, f32[16,128,64]{1,2,0:T(8,128)S(1)}, u32[]{:S(2)}, u32[]{:S(2)}) %collective-permute-start) | collective-permute-done | bytes 524320 | tf_op jit(solution)/shard_map/while/body/eval_jaxpr/ppermute | solution.py:17
  156.0 1.7 fusion.35
  160.8 2.0 copy.49
  163.6 9.8 %psum.14 = f32[512]{0:T(512)S(1)} all-reduce(f32[512]{0:T(512)S(1)} %multiply_reduce_fusion.1), channel_id=1, replica_groups=mesh['ctx'=64,'head'=4] {'head'}, use_global_device_ids=true, to_apply=%region_9.10 | all-reduce | flops 512 | bytes 4096 | tf_op jit(solution)/shard_map/psum | solution.py:111
  173.4 7.1 %fusion.40 = f32[512,2048]{1,0:T(8,128)} fusion(bf16[1024,2048]{1,0:T(8,128)(2,1)} %all-gather.4.cloned.1.call-done, f32[1024]{0:T(1024)S(1)} %copy-done.15, f32[512]{0:T(512)S(1)} %add_rsqrt_fusion.1, f32[512,1024]{1,0:T(8,128)S(1)} %copy.49, bf16[512,1024]{1,0:T(8,128)(2,1)S(1)} %copy-done.3), kind=kOutput, calls=%fused_computation.68 | convolution fusion | flops 2152202240 | bytes 11540480 | tf_op jit(solution)/shard_map/dot_general | solution.py:115
  180.5 2.5 add_dynamic-update-slice_fusion
  183.0 67.1 %all-reduce.1 = bf16[512,2048]{1,0:T(8,128)(2,1)S(1)} all-reduce(f32[512,2048]{1,0:T(8,128)} %add_dynamic-update-slice_fusion), channel_id=1, replica_groups=mesh['ctx'=64,'head'=4] {'head'}, use_global_device_ids=true, to_apply=%region_10.11 | all-reduce | flops 1048576 | bytes 6291456 | tf_op jit(solution)/shard_map/psum | solution.py:125
  250.8 5.9 %fusion.26 = f32[512,1024]{1,0:T(8,128)} fusion(bf16[2048,2048]{1,0:T(8,128)(2,1)} %all-gather.6.cloned.1.call-done, bf16[512,2048]{1,0:T(8,128)(2,1)S(1)} %all-reduce.1, f32[2048]{0:T(1024)S(1)} %copy-done.14, f32[512]{0:T(512)S(1)} %add_rsqrt_fusion), kind=kOutput, calls=%fused_computation.49 | convolution fusion | flops 2151677952 | bytes 8398848 | tf_op jit(solution)/shard_map/dot_general | solution.py:132
  258.0 10.0 %convolution_convert_fusion = bf16[512,2048]{1,0:T(8,128)(2,1)} fusion(bf16[1024,2048]{1,0:T(8,128)(2,1)} %all-gather.8.cloned.1.call-done, f32[512,1024]{1,0:T(8,128)} %fusion.26, bf16[2048,2048]{1,0:T(8,128)(2,1)} %all-gather.6.cloned.1.call-done, bf16[512,2048]{1,0:T(8,128)(2,1)S(1)} %all-reduce.1, f32[2048]{0:T(1024)S(1)} %copy-done.14, ...), kind=kOutput, calls=%fused_computation.51 | convolution fusion | flops 4303355904 | bytes 14690304 | tf_op jit(solution)/shard_map/dot_general | solution.py:136
  268.0 49.5 %reduce-scatter.2.cloned.1.call-done = bf16[512,512]{1,0:T(8,128)(2,1)} async-done(((bf16[512,2048]{1,0:T(8,128)(2,1)}), bf16[512,512]{1,0:T(8,128)(2,1)}) %reduce-scatter.2.cloned.1.call-update) | async-done | bytes 524304 | tf_op jit(solution)/shard_map/reduce_scatter | solution.py:141
  317.6 2.0 multiply_convert_fusion.5
  (146 shorter events, 37.3 us)
Async XLA Ops:
  6.5 8.5 %copy-start = (bf16[512,128]{1,0:T(8,128)(2,1)S(1)}, bf16[512,128]{1,0:T(8,128)(2,1)}, u32[]{:S(2)}) copy-start(bf16[512,128]{1,0:T(8,128)(2,1)} %param.21) | copy-start | bytes 393220
  6.5 166.8 %all-gather.4.cloned.1.call-start = ((), (), s32[]{:S(2)}) async-start(), calls=%async_computation.1 | async-start | bytes 4259840 | tf_op jit(solution)/shard_map/all_gather | solution.py:117
  7.3 243.3 %all-gather.6.cloned.1.call-start = ((), (), s32[]{:S(2)}) async-start(), calls=%async_computation.2 | async-start | bytes 8519680 | tf_op jit(solution)/shard_map/all_gather | solution.py:23
  8.9 249.2 %all-gather.8.cloned.1.call-start = ((), (), s32[]{:S(2)}) async-start(), calls=%async_computation.3 | async-start | bytes 4259840 | tf_op jit(solution)/shard_map/all_gather | solution.py:138
  9.6 308.0 %reduce-scatter.2.cloned.1.call-start = ((), (), s32[]{:S(2)}) async-start(), calls=%async_computation.4 | async-start | bytes 2621440 | tf_op jit(solution)/shard_map/reduce_scatter | solution.py:141
  21.8 3.2 copy-start.7
  21.8 4.5 %copy-start.4 = (f32[2,2,8,128]{3,2,0,1:T(8,128)S(1)}, f32[2,2,8,128]{3,2,0,1:T(8,128)}, u32[]{:S(2)}) copy-start(f32[2,2,8,128]{3,2,0,1:T(8,128)} %copy.65) | copy-start | bytes 49156 | tf_op jit(solution)/shard_map/while
  21.9 6.3 %copy-start.12 = (f32[2,16]{1,0:T(2,128)S(1)}, f32[2,16]{1,0:T(2,128)}, u32[]{:S(2)}) copy-start(f32[2,16]{1,0:T(2,128)} %get-tuple-element.291) | copy-start | bytes 388 | tf_op jit(solution)/shard_map/while
  21.9 6.4 %copy-start.2 = (f32[16,2,128]{2,0,1:T(8,128)S(1)}, f32[16,2,128]{2,0,1:T(8,128)}, u32[]{:S(2)}) copy-start(f32[16,2,128]{2,0,1:T(8,128)} %get-tuple-element.266) | copy-start | bytes 49156 | tf_op jit(solution)/shard_map/while
  21.9 6.4 %copy-start.8 = (f32[256]{0:T(256)S(1)}, f32[256]{0:T(256)}, u32[]{:S(2)}) copy-start(f32[256]{0:T(256)} %get-tuple-element.267) | copy-start | bytes 3076 | tf_op jit(solution)/shard_map/while
  21.9 6.4 %copy-start.9 = (f32[2,16,256]{2,1,0:T(8,128)S(1)}, f32[2,16,256]{2,1,0:T(8,128)}, u32[]{:S(2)}) copy-start(f32[2,16,256]{2,1,0:T(8,128)} %get-tuple-element.290) | copy-start | bytes 98308 | tf_op jit(solution)/shard_map/while
  33.7 1.8 copy-start.6
  35.7 3.2 copy-start.7
  35.7 4.6 %copy-start.4 = (f32[2,2,8,128]{3,2,0,1:T(8,128)S(1)}, f32[2,2,8,128]{3,2,0,1:T(8,128)}, u32[]{:S(2)}) copy-start(f32[2,2,8,128]{3,2,0,1:T(8,128)} %copy.65) | copy-start | bytes 49156 | tf_op jit(solution)/shard_map/while
  35.7 6.3 %copy-start.12 = (f32[2,16]{1,0:T(2,128)S(1)}, f32[2,16]{1,0:T(2,128)}, u32[]{:S(2)}) copy-start(f32[2,16]{1,0:T(2,128)} %get-tuple-element.291) | copy-start | bytes 388 | tf_op jit(solution)/shard_map/while
  35.7 6.4 %copy-start.2 = (f32[16,2,128]{2,0,1:T(8,128)S(1)}, f32[16,2,128]{2,0,1:T(8,128)}, u32[]{:S(2)}) copy-start(f32[16,2,128]{2,0,1:T(8,128)} %get-tuple-element.266) | copy-start | bytes 49156 | tf_op jit(solution)/shard_map/while
  35.7 6.4 %copy-start.8 = (f32[256]{0:T(256)S(1)}, f32[256]{0:T(256)}, u32[]{:S(2)}) copy-start(f32[256]{0:T(256)} %get-tuple-element.267) | copy-start | bytes 3076 | tf_op jit(solution)/shard_map/while
  35.7 6.4 %copy-start.9 = (f32[2,16,256]{2,1,0:T(8,128)S(1)}, f32[2,16,256]{2,1,0:T(8,128)}, u32[]{:S(2)}) copy-start(f32[2,16,256]{2,1,0:T(8,128)} %get-tuple-element.290) | copy-start | bytes 98308 | tf_op jit(solution)/shard_map/while
  45.4 11.2 %collective-permute-start = (f32[16,128,64]{1,2,0:T(8,128)S(1)}, f32[16,128,64]{1,2,0:T(8,128)S(1)}, u32[]{:S(2)}, u32[]{:S(2)}) collective-permute-start(f32[16,128,64]{1,2,0:T(8,128)S(1)} %multiply_add_fusion.2), channel_id=1, source_target_pairs={{0,4},{4,8},{8,12},{12,16},{16,20},{20,24},{24,28},{28,32},{32,36}... | collective-permute-start | bytes 1572872 | tf_op jit(solution)/shard_map/while/body/eval_jaxpr/ppermute | solution.py:17
  56.7 12.5 %collective-permute-start = (f32[16,128,64]{1,2,0:T(8,128)S(1)}, f32[16,128,64]{1,2,0:T(8,128)S(1)}, u32[]{:S(2)}, u32[]{:S(2)}) collective-permute-start(f32[16,128,64]{1,2,0:T(8,128)S(1)} %multiply_add_fusion.2), channel_id=1, source_target_pairs={{0,4},{4,8},{8,12},{12,16},{16,20},{20,24},{24,28},{28,32},{32,36}... | collective-permute-start | bytes 1572872 | tf_op jit(solution)/shard_map/while/body/eval_jaxpr/ppermute | solution.py:17
  69.3 15.2 %collective-permute-start = (f32[16,128,64]{1,2,0:T(8,128)S(1)}, f32[16,128,64]{1,2,0:T(8,128)S(1)}, u32[]{:S(2)}, u32[]{:S(2)}) collective-permute-start(f32[16,128,64]{1,2,0:T(8,128)S(1)} %multiply_add_fusion.2), channel_id=1, source_target_pairs={{0,4},{4,8},{8,12},{12,16},{16,20},{20,24},{24,28},{28,32},{32,36}... | collective-permute-start | bytes 1572872 | tf_op jit(solution)/shard_map/while/body/eval_jaxpr/ppermute | solution.py:17
  84.6 10.8 %collective-permute-start = (f32[16,128,64]{1,2,0:T(8,128)S(1)}, f32[16,128,64]{1,2,0:T(8,128)S(1)}, u32[]{:S(2)}, u32[]{:S(2)}) collective-permute-start(f32[16,128,64]{1,2,0:T(8,128)S(1)} %multiply_add_fusion.2), channel_id=1, source_target_pairs={{0,4},{4,8},{8,12},{12,16},{16,20},{20,24},{24,28},{28,32},{32,36}... | collective-permute-start | bytes 1572872 | tf_op jit(solution)/shard_map/while/body/eval_jaxpr/ppermute | solution.py:17
  95.4 10.5 %collective-permute-start = (f32[16,128,64]{1,2,0:T(8,128)S(1)}, f32[16,128,64]{1,2,0:T(8,128)S(1)}, u32[]{:S(2)}, u32[]{:S(2)}) collective-permute-start(f32[16,128,64]{1,2,0:T(8,128)S(1)} %multiply_add_fusion.2), channel_id=1, source_target_pairs={{0,4},{4,8},{8,12},{12,16},{16,20},{20,24},{24,28},{28,32},{32,36}... | collective-permute-start | bytes 1572872 | tf_op jit(solution)/shard_map/while/body/eval_jaxpr/ppermute | solution.py:17
  106.1 12.2 %collective-permute-start = (f32[16,128,64]{1,2,0:T(8,128)S(1)}, f32[16,128,64]{1,2,0:T(8,128)S(1)}, u32[]{:S(2)}, u32[]{:S(2)}) collective-permute-start(f32[16,128,64]{1,2,0:T(8,128)S(1)} %multiply_add_fusion.2), channel_id=1, source_target_pairs={{0,4},{4,8},{8,12},{12,16},{16,20},{20,24},{24,28},{28,32},{32,36}... | collective-permute-start | bytes 1572872 | tf_op jit(solution)/shard_map/while/body/eval_jaxpr/ppermute | solution.py:17
  118.3 12.0 %collective-permute-start = (f32[16,128,64]{1,2,0:T(8,128)S(1)}, f32[16,128,64]{1,2,0:T(8,128)S(1)}, u32[]{:S(2)}, u32[]{:S(2)}) collective-permute-start(f32[16,128,64]{1,2,0:T(8,128)S(1)} %multiply_add_fusion.2), channel_id=1, source_target_pairs={{0,4},{4,8},{8,12},{12,16},{16,20},{20,24},{24,28},{28,32},{32,36}... | collective-permute-start | bytes 1572872 | tf_op jit(solution)/shard_map/while/body/eval_jaxpr/ppermute | solution.py:17
  130.4 10.5 %collective-permute-start = (f32[16,128,64]{1,2,0:T(8,128)S(1)}, f32[16,128,64]{1,2,0:T(8,128)S(1)}, u32[]{:S(2)}, u32[]{:S(2)}) collective-permute-start(f32[16,128,64]{1,2,0:T(8,128)S(1)} %multiply_add_fusion.2), channel_id=1, source_target_pairs={{0,4},{4,8},{8,12},{12,16},{16,20},{20,24},{24,28},{28,32},{32,36}... | collective-permute-start | bytes 1572872 | tf_op jit(solution)/shard_map/while/body/eval_jaxpr/ppermute | solution.py:17
  141.1 15.0 %collective-permute-start = (f32[16,128,64]{1,2,0:T(8,128)S(1)}, f32[16,128,64]{1,2,0:T(8,128)S(1)}, u32[]{:S(2)}, u32[]{:S(2)}) collective-permute-start(f32[16,128,64]{1,2,0:T(8,128)S(1)} %multiply_add_fusion.2), channel_id=1, source_target_pairs={{0,4},{4,8},{8,12},{12,16},{16,20},{20,24},{24,28},{28,32},{32,36}... | collective-permute-start | bytes 1572872 | tf_op jit(solution)/shard_map/while/body/eval_jaxpr/ppermute | solution.py:17
  156.0 2.0 copy-start.1
  160.8 2.1 copy-start.3
  162.8 10.5 %copy-start.15 = (f32[1024]{0:T(1024)S(1)}, f32[1024]{0:T(1024)}, u32[]{:S(2)}) copy-start(f32[1024]{0:T(1024)} %param.27) | copy-start | bytes 12292
  173.4 7.1 %copy-start.5 = (bf16[512,512]{1,0:T(8,128)(2,1)S(1)}, bf16[512,512]{1,0:T(8,128)(2,1)}, u32[]{:S(2)}) copy-start(bf16[512,512]{1,0:T(8,128)(2,1)} %param.28) | copy-start | bytes 1572868
  268.0 49.6 %copy-start.11 = (f32[512]{0:T(512)S(1)}, f32[512]{0:T(512)}, u32[]{:S(2)}) copy-start(f32[512]{0:T(512)} %get-tuple-element.163) | copy-start | bytes 6148
  (6 other events, 4.8 us)
Sparse Core Ops, SparseCore 0:
  10.1 83.8 all-gather.3
  96.8 82.1 all-gather.5
  181.7 76.2 all-gather.7
  268.2 49.3 reduce-scatter.1
where the time goes:
time: 327 us; the launch traced here: 326 us
  waiting for transfers between devices  122 us (37%)
  blocking collectives  76.9 us (24%)
  starting transfers between devices  40.3 us (12%)
  matrix products  35.9 us (11%)
  other arithmetic  21.5 us (7%)
  local copies, waits for them, and re-layouts  14.6 us (4%)
  between operations  13.3 us (4%)
    ppermute x9, waiting for transfers between devices, passed_along(): return lax.ppermute(array, axis, pairs)  69.4 us
    psum x1, blocking collectives, shards(): hidden_full = lax.psum(projected + placed, 'head').astype(jnp.bfloat16)  67.1 us
    reduce_scatter x1, waiting for transfers between devices, shards(): lax.psum_scatter(down_out.astype(jnp.bfloat16), 'head', scatter_dimension...  49.5 us
    ppermute x9, starting transfers between devices, passed_along(): return lax.ppermute(array, axis, pairs)  40.1 us
    dot_general x1, matrix products, shards(): jnp.dot(columns, lax.all_gather(down_weight, 'ctx', axis=0, tiled=True),...  9.99 us
    psum x1, blocking collectives, shards(): squares = lax.psum(jnp.sum(gated * gated, axis=1), 'head')  9.76 us
    dot_general x1, matrix products, shards(): jnp.dot(columns, lax.all_gather(out_weight, 'ctx', axis=0, tiled=True), p...  7.13 us
  transfers between devices with their start and end apart: 13, of which 11 were waited for; matrix products, arithmetic and copies ran while one was open for 18% of the time, Pallas kernels for 0%

commit v1 on v0

--- a/solution.py
+++ b/solution.py
@@ -122,7 +122,7 @@
     placed = lax.dynamic_update_slice_in_dim(
         jnp.zeros((tok_rows, width), jnp.float32), residual.astype(jnp.float32), offset, 1
     )
-    hidden_full = lax.psum(projected + placed, "head").astype(jnp.bfloat16)
+    hidden_full = jnp.sum(lax.all_gather(projected + placed, "head"), axis=0).astype(jnp.bfloat16)
     hidden_wide = hidden_full.astype(jnp.float32)
     row_scale = lax.rsqrt(jnp.mean(hidden_wide * hidden_wide, axis=1) + EPS)
     scaled = (hidden_wide * row_scale[:, None] * mlp_gain).astype(jnp.bfloat16)

time: 327 us -> 557 us (1.70)
  waiting for transfers between devices: 122 us -> 414 us
  blocking collectives: 76.9 us -> 8.54 us
  other arithmetic: 21.5 us -> 27.4 us
    all_gather x0 -> x1, waiting for transfers between devices: none -> 171 us  [shards(): lax.all_gather(projected + placed, 'head')]
    all_gather x1, waiting for transfers between devices: 0.02 us -> 78.7 us  [sent_together(): filled = lax.all_gather(both, axis, axis=dim, tiled=True)]
    all_gather x1, waiting for transfers between devices: 1.32 us -> 72.6 us  [shards(): lax.all_gather(down_weight, 'ctx', axis=0, tiled=True)]
    psum x1 -> x0, blocking collectives: 67.1 us -> none  [shards(): hidden_full = lax.psum(projected + placed, 'head').astype(jnp.bfloat16)]
    reduce_scatter x1, waiting for transfers between devices: 49.5 us -> 29.2 us  [shards(): lax.psum_scatter(down_out.astype(jnp.bfloat16), 'head', scatter_dimension...]
    reduce_sum x0 -> x1, other arithmetic: none -> 8.11 us  [shards(): jnp.sum(lax.all_gather(projected + placed, 'head'), axis=0)]
    ppermute x9, waiting for transfers between devices: 69.4 us -> 61.4 us  [passed_along(): return lax.ppermute(array, axis, pairs)]
  transfers between devices with their start and end apart: 13 -> 14, of which waited for: 11 -> 13; matrix products, arithmetic and copies ran while one was open for 18% -> 10% of each run, Pallas kernels for 0% -> 0%
where the time goes in v1:
time: 557 us; the launch traced here: 556 us
  waiting for transfers between devices  414 us (74%)
  starting transfers between devices  40.5 us (7%)
  matrix products  33.7 us (6%)
  other arithmetic  27.4 us (5%)
  local copies, waits for them, and re-layouts  17.1 us (3%)
  between operations  13.3 us (2%)
  blocking collectives  8.54 us (2%)
    all_gather x1, waiting for transfers between devices, shards(): lax.all_gather(projected + placed, 'head')  171 us
    all_gather x1, waiting for transfers between devices, sent_together(): filled = lax.all_gather(both, axis, axis=dim, tiled=True)  78.7 us
    all_gather x1, waiting for transfers between devices, shards(): lax.all_gather(down_weight, 'ctx', axis=0, tiled=True)  72.6 us
    ppermute x9, waiting for transfers between devices, passed_along(): return lax.ppermute(array, axis, pairs)  61.4 us
    ppermute x9, starting transfers between devices, passed_along(): return lax.ppermute(array, axis, pairs)  40.1 us
    reduce_scatter x1, waiting for transfers between devices, shards(): lax.psum_scatter(down_out.astype(jnp.bfloat16), 'head', scatter_dimension...  29.2 us
  transfers between devices with their start and end apart: 14, of which 13 were waited for; matrix products, arithmetic and copies ran while one was open for 10% of the time, Pallas kernels for 0%

profile of v1, /device:TPU:1, one launch (start us, length us, event | category | flops | bytes accessed | tf_op | source)
XLA Modules:
  0.0 556.1 jit_solution(13999388936519057593)
XLA Ops:
  12.7 27.5 %while.26 = (s32[]{:T(128)}, f32[2,256,16,64]{1,3,2,0:T(8,128)}, f32[2,16,128,64]{2,3,1,0:T(8,128)S(1)}, f32[2,16,256]{2,1,0:T(8,128)}, f32[2,16]{1,0:T(2,128)},...) while((s32[]{:T(128)}, f32[2,256,16,64]{1,3,2,0:T(8,128)}, ...), condition=%wide.region_5.6_spmd, body=%wide.region_0.5_spmd.sunk | while | flops 225981504 | bytes 7140167 | solution.py:84
  19.5 3.2 fusion.76
  33.3 3.1 fusion.76
  42.7 102.8 %while.27 = (s32[]{:T(128)}, f32[16,128,64]{1,2,0:T(8,128)S(1)}, f32[16]{0:T(128)S(1)}, f32[16,128,64]{1,2,0:T(8,128)S(1)}, s32[]{:T(128)}) while((s32[]{:T(128)}, f32[16,128,64]{1,2,0:T(8,128)S(1)}, f32[16]{0:T(128)S(1)}, f32[16,128,64]{1,2,0:T(8,128)S(1)}, s32[]{:T(128)}) %tuple.50), condition=%wide.region_7.8_spmd, body=%wide.region_6.7_spmd.sunk | while | flops 262146 | bytes 3670181 | solution.py:99
  42.8 4.9 collective-permute-start
  47.7 6.3 %collective-permute-done = f32[16,128,64]{1,2,0:T(8,128)S(1)} collective-permute-done((f32[16,128,64]{1,2,0:T(8,128)S(1)}, f32[16,128,64]{1,2,0:T(8,128)S(1)}, u32[]{:S(2)}, u32[]{:S(2)}) %collective-permute-start) | collective-permute-done | bytes 524320 | tf_op jit(solution)/shard_map/while/body/eval_jaxpr/ppermute | solution.py:17
  54.1 4.4 collective-permute-start
  58.5 7.5 %collective-permute-done = f32[16,128,64]{1,2,0:T(8,128)S(1)} collective-permute-done((f32[16,128,64]{1,2,0:T(8,128)S(1)}, f32[16,128,64]{1,2,0:T(8,128)S(1)}, u32[]{:S(2)}, u32[]{:S(2)}) %collective-permute-start) | collective-permute-done | bytes 524320 | tf_op jit(solution)/shard_map/while/body/eval_jaxpr/ppermute | solution.py:17
  66.1 4.4 collective-permute-start
  70.5 9.6 %collective-permute-done = f32[16,128,64]{1,2,0:T(8,128)S(1)} collective-permute-done((f32[16,128,64]{1,2,0:T(8,128)S(1)}, f32[16,128,64]{1,2,0:T(8,128)S(1)}, u32[]{:S(2)}, u32[]{:S(2)}) %collective-permute-start) | collective-permute-done | bytes 524320 | tf_op jit(solution)/shard_map/while/body/eval_jaxpr/ppermute | solution.py:17
  80.3 4.5 collective-permute-start
  84.8 7.5 %collective-permute-done = f32[16,128,64]{1,2,0:T(8,128)S(1)} collective-permute-done((f32[16,128,64]{1,2,0:T(8,128)S(1)}, f32[16,128,64]{1,2,0:T(8,128)S(1)}, u32[]{:S(2)}, u32[]{:S(2)}) %collective-permute-start) | collective-permute-done | bytes 524320 | tf_op jit(solution)/shard_map/while/body/eval_jaxpr/ppermute | solution.py:17
  92.4 4.4 collective-permute-start
  96.8 6.1 %collective-permute-done = f32[16,128,64]{1,2,0:T(8,128)S(1)} collective-permute-done((f32[16,128,64]{1,2,0:T(8,128)S(1)}, f32[16,128,64]{1,2,0:T(8,128)S(1)}, u32[]{:S(2)}, u32[]{:S(2)}) %collective-permute-start) | collective-permute-done | bytes 524320 | tf_op jit(solution)/shard_map/while/body/eval_jaxpr/ppermute | solution.py:17
  103.1 4.4 collective-permute-start
  107.5 6.1 %collective-permute-done = f32[16,128,64]{1,2,0:T(8,128)S(1)} collective-permute-done((f32[16,128,64]{1,2,0:T(8,128)S(1)}, f32[16,128,64]{1,2,0:T(8,128)S(1)}, u32[]{:S(2)}, u32[]{:S(2)}) %collective-permute-start) | collective-permute-done | bytes 524320 | tf_op jit(solution)/shard_map/while/body/eval_jaxpr/ppermute | solution.py:17
  113.7 4.4 collective-permute-start
  118.1 6.1 %collective-permute-done = f32[16,128,64]{1,2,0:T(8,128)S(1)} collective-permute-done((f32[16,128,64]{1,2,0:T(8,128)S(1)}, f32[16,128,64]{1,2,0:T(8,128)S(1)}, u32[]{:S(2)}, u32[]{:S(2)}) %collective-permute-start) | collective-permute-done | bytes 524320 | tf_op jit(solution)/shard_map/while/body/eval_jaxpr/ppermute | solution.py:17
  124.3 4.4 collective-permute-start
  128.7 6.1 %collective-permute-done = f32[16,128,64]{1,2,0:T(8,128)S(1)} collective-permute-done((f32[16,128,64]{1,2,0:T(8,128)S(1)}, f32[16,128,64]{1,2,0:T(8,128)S(1)}, u32[]{:S(2)}, u32[]{:S(2)}) %collective-permute-start) | collective-permute-done | bytes 524320 | tf_op jit(solution)/shard_map/while/body/eval_jaxpr/ppermute | solution.py:17
  134.9 4.4 collective-permute-start
  139.3 6.1 %collective-permute-done = f32[16,128,64]{1,2,0:T(8,128)S(1)} collective-permute-done((f32[16,128,64]{1,2,0:T(8,128)S(1)}, f32[16,128,64]{1,2,0:T(8,128)S(1)}, u32[]{:S(2)}, u32[]{:S(2)}) %collective-permute-start) | collective-permute-done | bytes 524320 | tf_op jit(solution)/shard_map/while/body/eval_jaxpr/ppermute | solution.py:17
  150.2 2.0 copy.49
  152.9 8.5 %psum.7 = f32[512]{0:T(512)S(1)} all-reduce(f32[512]{0:T(512)S(1)} %multiply_reduce_fusion.1), channel_id=1, replica_groups=mesh['ctx'=64,'head'=4] {'head'}, use_global_device_ids=true, to_apply=%region_9.10 | all-reduce | flops 512 | bytes 4096 | tf_op jit(solution)/shard_map/psum | solution.py:111
  161.5 5.0 fusion.40
  172.1 170.6 %all-gather.7.cloned.1.call-done = f32[4,512,2048]{2,1,0:T(8,128)} async-done(((f32[1,512,2048]{2,1,0:T(8,128)}), f32[4,512,2048]{2,1,0:T(8,128)}) %all-gather.7.cloned.1.call-update) | async-done | bytes 16777232 | tf_op jit(solution)/shard_map/all_gather | solution.py:125
  342.6 8.1 %reduce_sum.28 = bf16[512,2048]{1,0:T(8,128)(2,1)S(1)} reduce(f32[4,512,2048]{2,1,0:T(8,128)} %all-gather.7.cloned.1.call-done, f32[]{:T(128)} %constant.33.clone.1), dimensions={0}, to_apply=%region_10.11 | reduce | flops 3145728 | bytes 18874372 | tf_op jit(solution)/shard_map/reduce_sum | solution.py:125
  351.3 78.7 %all-gather.9.cloned.1.call-done = bf16[2048,2048]{1,0:T(8,128)(2,1)} async-done(((bf16[32,2048]{1,0:T(8,128)(2,1)}), bf16[2048,2048]{1,0:T(8,128)(2,1)}) %all-gather.9.cloned.1.call-update) | async-done | bytes 8388624 | tf_op jit(solution)/shard_map/all_gather | solution.py:23
  430.0 5.9 %fusion.26 = f32[512,1024]{1,0:T(8,128)} fusion(bf16[2048,2048]{1,0:T(8,128)(2,1)} %all-gather.9.cloned.1.call-done, bf16[512,2048]{1,0:T(8,128)(2,1)S(1)} %reduce_sum.28, f32[2048]{0:T(1024)S(1)} %copy-done.16, f32[512]{0:T(512)S(1)} %add_rsqrt_fusion), kind=kOutput, calls=%fused_computation.49 | convolution fusion | flops 2151677952 | bytes 8398848 | tf_op jit(solution)/shard_map/dot_general | solution.py:132
  435.8 72.6 %all-gather.11.cloned.1.call-done = bf16[1024,2048]{1,0:T(8,128)(2,1)} async-done(((bf16[16,2048]{1,0:T(8,128)(2,1)}), bf16[1024,2048]{1,0:T(8,128)(2,1)}) %all-gather.11.cloned.1.call-update) | async-done | bytes 4194320 | tf_op jit(solution)/shard_map/all_gather | solution.py:138
  508.4 10.0 %convolution_convert_fusion = bf16[512,2048]{1,0:T(8,128)(2,1)} fusion(bf16[1024,2048]{1,0:T(8,128)(2,1)} %all-gather.11.cloned.1.call-done, f32[512,1024]{1,0:T(8,128)} %fusion.26, bf16[2048,2048]{1,0:T(8,128)(2,1)} %all-gather.9.cloned.1.call-done, bf16[512,2048]{1,0:T(8,128)(2,1)S(1)} %reduce_sum.28, f32[2048]{0:T(1024)S(1)} %copy-done.16, ...), kind=kOutput, calls=%fused_computation.51 | convolution fusion | flops 4303355904 | bytes 14690304 | tf_op jit(solution)/shard_map/dot_general | solution.py:136
  518.4 29.2 %reduce-scatter.2.cloned.1.call-done = bf16[512,512]{1,0:T(8,128)(2,1)} async-done(((bf16[512,2048]{1,0:T(8,128)(2,1)}), bf16[512,512]{1,0:T(8,128)(2,1)}) %reduce-scatter.2.cloned.1.call-update) | async-done | bytes 524304 | tf_op jit(solution)/shard_map/reduce_scatter | solution.py:141
  (154 shorter events, 42.5 us)
Async XLA Ops:
  6.5 6.1 %copy-start = (bf16[512,128]{1,0:T(8,128)(2,1)S(1)}, bf16[512,128]{1,0:T(8,128)(2,1)}, u32[]{:S(2)}) copy-start(bf16[512,128]{1,0:T(8,128)(2,1)} %param.21) | copy-start | bytes 393220
  6.5 154.9 %all-gather.5.cloned.1.call-start = ((), (), s32[]{:S(2)}) async-start(), calls=%async_computation.1 | async-start | bytes 4259840 | tf_op jit(solution)/shard_map/all_gather | solution.py:117
  7.3 335.4 %all-gather.7.cloned.1.call-start = ((), (), s32[]{:S(2)}) async-start(), calls=%async_computation.2 | async-start | bytes 20971520 | tf_op jit(solution)/shard_map/all_gather | solution.py:125
  19.5 3.2 copy-start.7
  19.5 4.5 copy-start.4
  19.5 6.2 %copy-start.14 = (f32[2,16]{1,0:T(2,128)S(1)}, f32[2,16]{1,0:T(2,128)}, u32[]{:S(2)}) copy-start(f32[2,16]{1,0:T(2,128)} %get-tuple-element.291) | copy-start | bytes 388 | tf_op jit(solution)/shard_map/while
  19.5 6.3 %copy-start.2 = (f32[16,2,128]{2,0,1:T(8,128)S(1)}, f32[16,2,128]{2,0,1:T(8,128)}, u32[]{:S(2)}) copy-start(f32[16,2,128]{2,0,1:T(8,128)} %get-tuple-element.266) | copy-start | bytes 49156 | tf_op jit(solution)/shard_map/while
  19.5 6.3 %copy-start.8 = (f32[256]{0:T(256)S(1)}, f32[256]{0:T(256)}, u32[]{:S(2)}) copy-start(f32[256]{0:T(256)} %get-tuple-element.267) | copy-start | bytes 3076 | tf_op jit(solution)/shard_map/while
  19.5 6.3 %copy-start.11 = (f32[2,16,256]{2,1,0:T(8,128)S(1)}, f32[2,16,256]{2,1,0:T(8,128)}, u32[]{:S(2)}) copy-start(f32[2,16,256]{2,1,0:T(8,128)} %get-tuple-element.290) | copy-start | bytes 98308 | tf_op jit(solution)/shard_map/while
  33.2 3.2 copy-start.7
  33.2 4.4 copy-start.4
  33.2 6.2 %copy-start.14 = (f32[2,16]{1,0:T(2,128)S(1)}, f32[2,16]{1,0:T(2,128)}, u32[]{:S(2)}) copy-start(f32[2,16]{1,0:T(2,128)} %get-tuple-element.291) | copy-start | bytes 388 | tf_op jit(solution)/shard_map/while
  33.3 6.2 %copy-start.2 = (f32[16,2,128]{2,0,1:T(8,128)S(1)}, f32[16,2,128]{2,0,1:T(8,128)}, u32[]{:S(2)}) copy-start(f32[16,2,128]{2,0,1:T(8,128)} %get-tuple-element.266) | copy-start | bytes 49156 | tf_op jit(solution)/shard_map/while
  33.3 6.3 %copy-start.8 = (f32[256]{0:T(256)S(1)}, f32[256]{0:T(256)}, u32[]{:S(2)}) copy-start(f32[256]{0:T(256)} %get-tuple-element.267) | copy-start | bytes 3076 | tf_op jit(solution)/shard_map/while
  33.3 6.3 %copy-start.11 = (f32[2,16,256]{2,1,0:T(8,128)S(1)}, f32[2,16,256]{2,1,0:T(8,128)}, u32[]{:S(2)}) copy-start(f32[2,16,256]{2,1,0:T(8,128)} %get-tuple-element.290) | copy-start | bytes 98308 | tf_op jit(solution)/shard_map/while
  42.8 11.2 %collective-permute-start = (f32[16,128,64]{1,2,0:T(8,128)S(1)}, f32[16,128,64]{1,2,0:T(8,128)S(1)}, u32[]{:S(2)}, u32[]{:S(2)}) collective-permute-start(f32[16,128,64]{1,2,0:T(8,128)S(1)} %multiply_add_fusion.2), channel_id=1, source_target_pairs={{0,4},{4,8},{8,12},{12,16},{16,20},{20,24},{24,28},{28,32},{32,36}... | collective-permute-start | bytes 1572872 | tf_op jit(solution)/shard_map/while/body/eval_jaxpr/ppermute | solution.py:17
  54.1 11.9 %collective-permute-start = (f32[16,128,64]{1,2,0:T(8,128)S(1)}, f32[16,128,64]{1,2,0:T(8,128)S(1)}, u32[]{:S(2)}, u32[]{:S(2)}) collective-permute-start(f32[16,128,64]{1,2,0:T(8,128)S(1)} %multiply_add_fusion.2), channel_id=1, source_target_pairs={{0,4},{4,8},{8,12},{12,16},{16,20},{20,24},{24,28},{28,32},{32,36}... | collective-permute-start | bytes 1572872 | tf_op jit(solution)/shard_map/while/body/eval_jaxpr/ppermute | solution.py:17
  66.1 14.0 %collective-permute-start = (f32[16,128,64]{1,2,0:T(8,128)S(1)}, f32[16,128,64]{1,2,0:T(8,128)S(1)}, u32[]{:S(2)}, u32[]{:S(2)}) collective-permute-start(f32[16,128,64]{1,2,0:T(8,128)S(1)} %multiply_add_fusion.2), channel_id=1, source_target_pairs={{0,4},{4,8},{8,12},{12,16},{16,20},{20,24},{24,28},{28,32},{32,36}... | collective-permute-start | bytes 1572872 | tf_op jit(solution)/shard_map/while/body/eval_jaxpr/ppermute | solution.py:17
  80.3 12.0 %collective-permute-start = (f32[16,128,64]{1,2,0:T(8,128)S(1)}, f32[16,128,64]{1,2,0:T(8,128)S(1)}, u32[]{:S(2)}, u32[]{:S(2)}) collective-permute-start(f32[16,128,64]{1,2,0:T(8,128)S(1)} %multiply_add_fusion.2), channel_id=1, source_target_pairs={{0,4},{4,8},{8,12},{12,16},{16,20},{20,24},{24,28},{28,32},{32,36}... | collective-permute-start | bytes 1572872 | tf_op jit(solution)/shard_map/while/body/eval_jaxpr/ppermute | solution.py:17
  92.4 10.5 %collective-permute-start = (f32[16,128,64]{1,2,0:T(8,128)S(1)}, f32[16,128,64]{1,2,0:T(8,128)S(1)}, u32[]{:S(2)}, u32[]{:S(2)}) collective-permute-start(f32[16,128,64]{1,2,0:T(8,128)S(1)} %multiply_add_fusion.2), channel_id=1, source_target_pairs={{0,4},{4,8},{8,12},{12,16},{16,20},{20,24},{24,28},{28,32},{32,36}... | collective-permute-start | bytes 1572872 | tf_op jit(solution)/shard_map/while/body/eval_jaxpr/ppermute | solution.py:17
  103.1 10.5 %collective-permute-start = (f32[16,128,64]{1,2,0:T(8,128)S(1)}, f32[16,128,64]{1,2,0:T(8,128)S(1)}, u32[]{:S(2)}, u32[]{:S(2)}) collective-permute-start(f32[16,128,64]{1,2,0:T(8,128)S(1)} %multiply_add_fusion.2), channel_id=1, source_target_pairs={{0,4},{4,8},{8,12},{12,16},{16,20},{20,24},{24,28},{28,32},{32,36}... | collective-permute-start | bytes 1572872 | tf_op jit(solution)/shard_map/while/body/eval_jaxpr/ppermute | solution.py:17
  113.7 10.5 %collective-permute-start = (f32[16,128,64]{1,2,0:T(8,128)S(1)}, f32[16,128,64]{1,2,0:T(8,128)S(1)}, u32[]{:S(2)}, u32[]{:S(2)}) collective-permute-start(f32[16,128,64]{1,2,0:T(8,128)S(1)} %multiply_add_fusion.2), channel_id=1, source_target_pairs={{0,4},{4,8},{8,12},{12,16},{16,20},{20,24},{24,28},{28,32},{32,36}... | collective-permute-start | bytes 1572872 | tf_op jit(solution)/shard_map/while/body/eval_jaxpr/ppermute | solution.py:17
  124.3 10.5 %collective-permute-start = (f32[16,128,64]{1,2,0:T(8,128)S(1)}, f32[16,128,64]{1,2,0:T(8,128)S(1)}, u32[]{:S(2)}, u32[]{:S(2)}) collective-permute-start(f32[16,128,64]{1,2,0:T(8,128)S(1)} %multiply_add_fusion.2), channel_id=1, source_target_pairs={{0,4},{4,8},{8,12},{12,16},{16,20},{20,24},{24,28},{28,32},{32,36}... | collective-permute-start | bytes 1572872 | tf_op jit(solution)/shard_map/while/body/eval_jaxpr/ppermute | solution.py:17
  134.9 10.5 %collective-permute-start = (f32[16,128,64]{1,2,0:T(8,128)S(1)}, f32[16,128,64]{1,2,0:T(8,128)S(1)}, u32[]{:S(2)}, u32[]{:S(2)}) collective-permute-start(f32[16,128,64]{1,2,0:T(8,128)S(1)} %multiply_add_fusion.2), channel_id=1, source_target_pairs={{0,4},{4,8},{8,12},{12,16},{16,20},{20,24},{24,28},{28,32},{32,36}... | collective-permute-start | bytes 1572872 | tf_op jit(solution)/shard_map/while/body/eval_jaxpr/ppermute | solution.py:17
  150.2 2.0 copy-start.3
  152.2 9.3 %copy-start.17 = (f32[1024]{0:T(1024)S(1)}, f32[1024]{0:T(1024)}, u32[]{:S(2)}) copy-start(f32[1024]{0:T(1024)} %param.27) | copy-start | bytes 12292
  166.5 2.0 copy-start.5
  169.7 260.2 %all-gather.9.cloned.1.call-start = ((), (), s32[]{:S(2)}) async-start(), calls=%async_computation.3 | async-start | bytes 8519680 | tf_op jit(solution)/shard_map/all_gather | solution.py:23
  171.3 337.2 %all-gather.11.cloned.1.call-start = ((), (), s32[]{:S(2)}) async-start(), calls=%async_computation.4 | async-start | bytes 4259840 | tf_op jit(solution)/shard_map/all_gather | solution.py:138
  171.8 375.8 %reduce-scatter.2.cloned.1.call-start = ((), (), s32[]{:S(2)}) async-start(), calls=%async_computation.5 | async-start | bytes 2621440 | tf_op jit(solution)/shard_map/reduce_scatter | solution.py:141
  350.8 79.2 %copy-start.16 = (f32[2048]{0:T(1024)S(1)}, f32[2048]{0:T(1024)}, u32[]{:S(2)}) copy-start(f32[2048]{0:T(1024)} %param.30) | copy-start | bytes 24580
  518.4 29.2 %copy-start.13 = (f32[512]{0:T(512)S(1)}, f32[512]{0:T(512)}, u32[]{:S(2)}) copy-start(f32[512]{0:T(512)} %get-tuple-element.163) | copy-start | bytes 6148
  (9 other events, 9.6 us)
Sparse Core Ops, SparseCore 0:
  10.1 83.6 all-gather.4
  169.9 172.7 all-gather.6
  345.4 84.4 all-gather.8
  432.6 75.7 all-gather.10
  518.5 29.0 reduce-scatter.1
